TPU v7x, 32 devices: a whole 2x2x4 slice. The times are simulated.
32 devices in a mesh: seq: 8 (over z, x), exp: 4 (over y, core).
Axes of the slice: x: 2, y: 2, z: 4, core: 2. Of those that a mesh axis runs over, the one named last changes fastest.
Arguments:
- residual: bfloat16 [4096, 8192], P('seq', 'exp'), may hold values from -16 to 16
- queries: bfloat16 [4096, 4096], P('seq', 'exp'), may hold values from -6 to 6
- keys: bfloat16 [4096, 4096], P('seq', 'exp'), may hold values from -10 to 10
- values: bfloat16 [4096, 4096], P('seq', 'exp'), may hold values from -6 to 6
- documents: int32 [4096], replicated, may hold values from 0 to 1, as said below
- out_proj: bfloat16 [4096, 8192], P(None, 'exp'), may hold values from -0.09375 to 0.09375
- modality: int32 [4096], P('seq'), may hold values from 0 to 1, as said below
- norm_gain: float32 [2, 8192], P(None, 'exp'), may hold values from 0.25 to 1.75
- picks: int32 [4, 64], replicated, may hold values from 0 to 4095, as said below
- router: bfloat16 [8192, 4], P(None, 'exp'), may hold values from -0.0625 to 0.0625
- w_gate: bfloat16 [4, 8192, 4096], P('exp', None, 'seq'), may hold values from -0.0625 to 0.0625
- w_up: bfloat16 [4, 8192, 4096], P('exp', None, 'seq'), may hold values from -0.0625 to 0.0625
- w_down: bfloat16 [4, 4096, 8192], P('exp', 'seq'), may hold values from -0.09375 to 0.09375
Outputs:
- layer_out: bfloat16 [4096, 8192], P('seq', 'exp')
Inputs may be any that keep to these rules, and one draw needn't show every extreme that they name: `modality`: 0 marks a text token, 1 an image token. `documents`: 0 for the first document, 1 for the second; the second begins between position 1024 and 3072. `picks`: row e lists 64 different positions in ascending order; all carry modality 0 for e < 2 and modality 1 otherwise. Within each aligned block of 512 positions (the tokens of one index of seq) a row lists at most 16 positions, and every row lists exactly 16 in some block.
All inputs are finite; a program needn't handle non-finite values.
Results may differ from a plain program's by a relative error of at most 0.0035.
Values may be sent and summed in bfloat16 or wider, within the bound.
A program may use at most 128 MiB of HBM per device.

v0:
```python
import math

import jax
import jax.numpy as jnp
from jax import lax
from jax.sharding import PartitionSpec as P

D = 8192
HD = 128


block_rows = 512


def shards(
    residual,
    queries,
    keys,
    values,
    documents,
    out_proj,
    modality,
    norm_gain,
    picks,
    router,
    w_gate,
    w_up,
    w_down,
):
    tokens = queries.shape[0]
    heads_here = queries.shape[1] // HD
    seq_pos = lax.axis_index("seq")
    start_row = seq_pos * tokens
    query_pos = start_row + jnp.arange(tokens, dtype=jnp.int32)
    query_doc = lax.dynamic_slice_in_dim(documents, start_row, tokens, 0)
    query_heads = queries.reshape(tokens, heads_here, HD)
    score_scale = 1.0 / math.sqrt(HD)

    def attend(state, key_rows, value_rows, key_start):
        row_count = key_rows.shape[0]
        key_pos = key_start + jnp.arange(row_count, dtype=jnp.int32)
        key_doc = lax.dynamic_slice_in_dim(documents, key_start, row_count, 0)
        scores = (
            jnp.einsum(
                "qhd,khd->qhk",
                query_heads,
                key_rows.reshape(row_count, heads_here, HD),
                preferred_element_type=jnp.float32,
            )
            * score_scale
        )
        allowed = (key_pos[None, :] <= query_pos[:, None]) & (
            key_doc[None, :] == query_doc[:, None]
        )
        scores = jnp.where(allowed[:, None, :], scores, -jnp.inf)
        running_max, running_sum, running_out = state
        new_max = jnp.maximum(running_max, jnp.max(scores, axis=2))
        factor = jnp.exp(running_max - new_max)
        weights = jnp.exp(scores - new_max[:, :, None])
        running_sum = running_sum * factor + jnp.sum(weights, axis=2)
        running_out = running_out * factor[:, :, None] + jnp.einsum(
            "qhk,khd->qhd",
            weights.astype(jnp.bfloat16),
            value_rows.reshape(row_count, heads_here, HD),
            preferred_element_type=jnp.float32,
        )
        return (new_max, running_sum, running_out)

    def visit_block(state, key_rows, value_rows, key_start):
        row_count = key_rows.shape[0]
        last_doc = lax.dynamic_index_in_dim(documents, key_start + row_count - 1, 0, keepdims=False)
        beyond = (key_start > query_pos[tokens - 1]) | (last_doc < query_doc[0])
        return lax.cond(
            beyond,
            lambda inner_state: inner_state,
            lambda inner_state: attend(inner_state, key_rows, value_rows, key_start),
            state,
        )

    initial = (
        jnp.full((tokens, heads_here), -1e30, jnp.float32),
        jnp.zeros((tokens, heads_here), jnp.float32),
        jnp.zeros((tokens, heads_here, HD), jnp.float32),
    )
    state = initial
    key_piece = lax.all_gather(keys, "seq", axis=0, tiled=True)
    value_piece = lax.all_gather(values, "seq", axis=0, tiled=True)
    row_count = key_piece.shape[0]
    blocks = row_count // block_rows
    key_stack = key_piece.reshape(blocks, block_rows, key_piece.shape[1])
    value_stack = value_piece.reshape(blocks, block_rows, value_piece.shape[1])

    def scan_step(inner_state, block_item):
        block_index, key_rows, value_rows = block_item
        return (visit_block(inner_state, key_rows, value_rows, block_index * block_rows), None)

    state, unused = lax.scan(
        scan_step, state, (jnp.arange(blocks, dtype=jnp.int32), key_stack, value_stack)
    )
    running_max, running_sum, running_out = state
    attended = (
        (running_out / running_sum[:, :, None])
        .reshape(tokens, heads_here * HD)
        .astype(jnp.bfloat16)
    )
    mixed = jnp.dot(
        lax.all_gather(attended, "exp", axis=1, tiled=True),
        out_proj,
        preferred_element_type=jnp.float32,
    )
    hidden_state = (residual.astype(jnp.float32) + mixed).astype(jnp.bfloat16)
    hidden_wide = hidden_state.astype(jnp.float32)
    square_total = lax.psum(jnp.sum(hidden_wide * hidden_wide, axis=1), "exp")
    inverse = lax.rsqrt(square_total / D + 1e-05)
    gain_rows = jnp.where(modality[:, None] == 0, norm_gain[0][None, :], norm_gain[1][None, :])
    normed = (hidden_wide * inverse[:, None] * gain_rows).astype(jnp.bfloat16)
    capacity = tokens // 32
    inside = (picks >= start_row) & (picks < start_row + tokens)
    slot_index = jnp.cumsum(inside.astype(jnp.int32), axis=1) - 1
    matched = inside[:, None, :] & (
        slot_index[:, None, :] == jnp.arange(capacity, dtype=jnp.int32)[None, :, None]
    )
    local_index = jnp.sum(jnp.where(matched, picks[:, None, :] - start_row, 0), axis=2)
    filled = jnp.any(matched, axis=2)
    rows_out = jnp.take(normed, local_index.T, axis=0)
    rows_out = jnp.where(filled.T[:, :, None], rows_out, jnp.zeros_like(rows_out))
    arrived = lax.all_to_all(rows_out, "exp", split_axis=1, concat_axis=1, tiled=True)
    expert_rows = arrived.reshape(capacity, D)
    logits = jnp.dot(expert_rows, router, preferred_element_type=jnp.float32)[:, 0]
    piece = lax.all_gather(expert_rows, "seq", axis=0, tiled=True)
    gate_part = jnp.dot(piece, w_gate[0], preferred_element_type=jnp.float32)
    up_part = jnp.dot(piece, w_up[0], preferred_element_type=jnp.float32)
    inner_act = (jax.nn.silu(gate_part) * up_part).astype(jnp.bfloat16)
    summed = lax.psum_scatter(
        jnp.dot(inner_act, w_down[0], preferred_element_type=jnp.float32).astype(jnp.bfloat16),
        "seq",
        scatter_dimension=0,
        tiled=True,
    ).astype(jnp.float32)
    weighted = (jax.nn.sigmoid(logits)[:, None] * summed).astype(jnp.bfloat16)
    own_expert = lax.axis_index("exp")
    own_index = lax.dynamic_index_in_dim(local_index, own_expert, 0, keepdims=False)
    own_filled = lax.dynamic_index_in_dim(filled, own_expert, 0, keepdims=False)
    placing = (
        (jnp.arange(tokens, dtype=jnp.int32)[:, None] == own_index[None, :]) & own_filled[None, :]
    ).astype(jnp.bfloat16)
    spread = jnp.dot(placing, weighted, preferred_element_type=jnp.float32)
    expert_add = lax.psum_scatter(
        spread.astype(jnp.bfloat16), "exp", scatter_dimension=1, tiled=True
    ).astype(jnp.float32)
    return (hidden_wide + expert_add).astype(jnp.bfloat16)


def solution(mesh):
    return jax.shard_map(
        shards,
        mesh=mesh,
        in_specs=(
            P("seq", "exp"),
            P("seq", "exp"),
            P("seq", "exp"),
            P("seq", "exp"),
            P(),
            P(None, "exp"),
            P("seq"),
            P(None, "exp"),
            P(),
            P(None, "exp"),
            P("exp", None, "seq"),
            P("exp", None, "seq"),
            P("exp", "seq", None),
        ),
        out_specs=P("seq", "exp"),
        check_vma=False,
    )
```

profile of v0, /device:TPU:0, one launch (start us, length us, event | category | flops | bytes accessed | tf_op | source)
XLA Modules:
  0.0 667.6 jit_solution(14505423510101249050)
XLA Ops:
  8.1 1.5 copy.56
  11.0 125.7 %all-gather.5.cloned.1.call-done = bf16[4096,1024]{1,0:T(8,128)(2,1)} async-done(((bf16[512,1024]{1,0:T(8,128)(2,1)}), bf16[4096,1024]{1,0:T(8,128)(2,1)}) %all-gather.5.cloned.1.call-update) | async-done | bytes 8388624 | tf_op jit(solution)/shard_map/all_gather | solution.py:86
  136.7 11.6 %copy.57 = bf16[8,512,1024]{1,2,0:T(8,128)(2,1)} copy(bf16[8,512,1024]{2,1,0:T(8,128)(2,1)} %bitcast.77) | data formatting | bytes 16777216 | tf_op jit(solution)/shard_map/while | solution.py:97
  148.3 113.2 %all-gather.7.cloned.1.call-done = bf16[4096,1024]{1,0:T(8,128)(2,1)} async-done(((bf16[512,1024]{1,0:T(8,128)(2,1)}), bf16[4096,1024]{1,0:T(8,128)(2,1)}) %all-gather.7.cloned.1.call-update) | async-done | bytes 8388624 | tf_op jit(solution)/shard_map/all_gather | solution.py:87
  261.5 11.4 %copy.59 = bf16[8,512,1024]{1,2,0:T(8,128)(2,1)} copy(bf16[8,512,1024]{2,1,0:T(8,128)(2,1)} %bitcast.78) | data formatting | bytes 16777216 | tf_op jit(solution)/shard_map/while | solution.py:97
  273.1 55.4 %while.18 = (s32[]{:T(128)}, f32[512,8]{0,1:T(8,128)S(1)}, f32[512,8]{0,1:T(8,128)S(1)}, f32[512,8,128]{2,0,1:T(8,128)S(1)}, s32[8]{0:T(128)S(1)}, /*index=5*/s3...) while((s32[]{:T(128)}, f32[512,8]{0,1:T(8,128)S(1)}, ...), condition=%wide.region_5.6_spmd, body=%wide.region_0.5_spmd.sunk | while | flops 1098654208 | bytes 38025672 | solution.py:97
  274.4 1.3 dynamic_slice.65
  278.7 9.6 %conditional.2 = (f32[512,8]{0,1:T(8,128)S(1)}, f32[512,8]{0,1:T(8,128)S(1)}, f32[512,8,128]{2,0,1:T(8,128)S(1)}) conditional(s32[]{:T(128)} %convert_element_type.103, (s32[]{:T(128)}, s32[512]{0:T(512)S(1)}, s32[4096]{0:T(1024)}, s32[512]{0:T(512)S(1)}, bf16[8,512,1024]{1,2,0:T(8,128)(2,1)}, /*index=5*/s32[]{:T(128)}, ...), branch_computations={%region_1.3_spmd, %region_4.4_spmd} | conditional | flops 1098654208 | bytes 37992520 | solution.py:73
  279.8 1.7 constant_dynamic-slice_fusion
  281.5 1.7 fusion.2
  283.2 1.7 fusion.1
  285.0 3.4 bitcast_add_fusion
  289.6 1.3 dynamic_slice.65
  295.4 1.3 dynamic_slice.65
  301.1 1.3 dynamic_slice.65
  306.8 1.3 dynamic_slice.65
  312.6 1.3 dynamic_slice.65
  328.5 1.8 copy.60
  330.3 2.8 divide_convert_fusion
  334.3 79.5 %all-gather.9.cloned.1.call-done = bf16[512,4096]{0,1:T(8,128)(2,1)} async-done(((bf16[512,1024]{0,1:T(8,128)(2,1)}), bf16[512,4096]{0,1:T(8,128)(2,1)}) %all-gather.9.cloned.1.call-update) | async-done | bytes 4194320 | tf_op jit(solution)/shard_map/all_gather | solution.py:107
  413.8 14.2 %fusion.18 = (f32[512]{0:T(512)S(1)}, bf16[512,2048]{1,0:T(8,128)(2,1)S(1)}) fusion(bf16[512,4096]{0,1:T(8,128)(2,1)} %all-gather.9.cloned.1.call-done, bf16[4096,2048]{1,0:T(8,128)(2,1)} %param.22, bf16[512,2048]{1,0:T(8,128)(2,1)} %param.17), kind=kOutput, calls=%fused_computation.30 | convolution fusion | flops 8596226048 | bytes 25167872 | tf_op jit(solution)/shard_map/dot_general | solution.py:106
  428.0 5.9 psum.7
  433.9 2.1 fusion.20
  436.0 2.8 gather_fusion
  439.3 8.7 %all_to_all.5 = bf16[16,4,2048]{2,0,1:T(8,128)(2,1)S(1)} all-to-all(bf16[16,4,2048]{2,0,1:T(8,128)(2,1)S(1)} %fusion.34), channel_id=1, replica_groups=mesh['seq'=8,'exp'=4] {'exp'}, dimensions={1} | all-to-all | bytes 524288 | tf_op jit(solution)/shard_map/all_to_all | solution.py:127
  448.8 49.2 %all-gather.11.cloned.1.call-done = bf16[128,8192]{1,0:T(8,128)(2,1)} async-done(((bf16[16,8192]{1,0:T(8,128)(2,1)}), bf16[128,8192]{1,0:T(8,128)(2,1)}) %all-gather.11.cloned.1.call-update) | async-done | bytes 2097168 | tf_op jit(solution)/shard_map/all_gather | solution.py:130
  498.0 5.4 fusion.16
  503.5 9.6 %convolution_convert_fusion.1 = bf16[128,8192]{1,0:T(8,128)(2,1)} fusion(bf16[1,512,8192]{2,1,0:T(8,128)(2,1)} %param.29, bf16[128,8192]{1,0:T(8,128)(2,1)S(1)} %copy-done.1, bf16[1,8192,512]{2,1,0:T(8,128)(2,1)} %param.28, f32[128,512]{1,0:T(8,128)S(1)} %fusion.16), kind=kOutput, calls=%fused_computation.21 | convolution fusion | flops 2148925440 | bytes 21233664 | tf_op jit(solution)/shard_map/dot_general | solution.py:135
  513.6 66.4 %reduce-scatter.3.cloned.1.call-done = bf16[16,8192]{1,0:T(8,128)(2,1)} async-done(((bf16[128,8192]{1,0:T(8,128)(2,1)}), bf16[16,8192]{1,0:T(8,128)(2,1)}) %reduce-scatter.3.cloned.1.call-update) | async-done | bytes 262160 | tf_op jit(solution)/shard_map/reduce_scatter | solution.py:134
  580.1 6.6 convolution_convert_fusion
  586.7 70.4 %reduce-scatter.5.cloned.1.call-done = bf16[512,2048]{1,0:T(8,128)(2,1)} async-done(((bf16[512,8192]{1,0:T(8,128)(2,1)}), bf16[512,2048]{1,0:T(8,128)(2,1)}) %reduce-scatter.5.cloned.1.call-update) | async-done | bytes 2097168 | tf_op jit(solution)/shard_map/reduce_scatter | solution.py:148
  657.1 3.7 fusion.21
  (107 shorter events, 24.3 us)
Async XLA Ops:
  6.5 506.9 %copy-start = (bf16[8192,1]{0,1:T(2,128)(2,1)S(1)}, bf16[8192,1]{0,1:T(2,128)(2,1)}, u32[]{:S(2)}) copy-start(bf16[8192,1]{0,1:T(2,128)(2,1)} %param.26) | copy-start | bytes 49156
  6.5 130.1 %all-gather.5.cloned.1.call-start = ((), (), s32[]{:S(2)}) async-start(), calls=%async_computation.3 | async-start | bytes 9437184 | tf_op jit(solution)/shard_map/all_gather | solution.py:86
  7.3 254.2 %all-gather.7.cloned.1.call-start = ((), (), s32[]{:S(2)}) async-start(), calls=%async_computation.4 | async-start | bytes 9437184 | tf_op jit(solution)/shard_map/all_gather | solution.py:87
  8.0 405.8 %all-gather.9.cloned.1.call-start = ((), (), s32[]{:S(2)}) async-start(), calls=%async_computation.5 | async-start | bytes 5242880 | tf_op jit(solution)/shard_map/all_gather | solution.py:107
  328.5 4.9 copy-start.6
  328.5 5.7 copy-start.7
  328.5 5.7 copy-start.5
  333.2 164.8 %all-gather.11.cloned.1.call-start = ((), (), s32[]{:S(2)}) async-start(), calls=%async_computation.6 | async-start | bytes 2359296 | tf_op jit(solution)/shard_map/all_gather | solution.py:130
  428.0 20.8 %copy-start.2 = (bf16[512,2048]{1,0:T(8,128)(2,1)}, bf16[512,2048]{1,0:T(8,128)(2,1)S(1)}, u32[]{:S(2)}) copy-start(bf16[512,2048]{1,0:T(8,128)(2,1)S(1)} %get-tuple-element.425) | copy-start | bytes 6291460
  448.8 131.3 %reduce-scatter.3.cloned.1.call-start = ((), (), s32[]{:S(2)}) async-start(), calls=%async_computation.7 | async-start | bytes 2359296 | tf_op jit(solution)/shard_map/reduce_scatter | solution.py:134
  498.0 5.4 copy-start.1
  503.5 10.0 %copy-start.4 = (bf16[4,2,8,2048]{3,2,0,1:T(8,128)(2,1)S(1)}, bf16[4,2,8,2048]{3,2,0,1:T(8,128)(2,1)}, u32[]{:S(2)}) copy-start(bf16[4,2,8,2048]{3,2,0,1:T(8,128)(2,1)} %copy.67) | copy-start | bytes 786436
  513.1 144.0 %reduce-scatter.5.cloned.1.call-start = ((), (), s32[]{:S(2)}) async-start(), calls=%async_computation.8 | async-start | bytes 10485760 | tf_op jit(solution)/shard_map/reduce_scatter | solution.py:148
  586.6 70.5 %copy-start.3 = (bf16[512,2048]{1,0:T(8,128)(2,1)S(1)}, bf16[512,2048]{1,0:T(8,128)(2,1)}, u32[]{:S(2)}) copy-start(bf16[512,2048]{1,0:T(8,128)(2,1)} %copy-done.2) | copy-start | bytes 6291460
Sparse Core Ops, SparseCore 0:
  9.5 127.1 all-gather.4
  138.8 122.6 all-gather.6
  333.3 80.4 all-gather.8
  448.9 49.0 all-gather.10
  513.2 66.7 reduce-scatter.2
  586.8 70.2 reduce-scatter.4
where the time goes:
time: 665 us; the launch traced here: 668 us
  waiting for transfers between devices  506 us (76%)
  local copies, waits for them, and re-layouts  59.3 us (9%)
  matrix products  41 us (6%)
  loops' own time  20.9 us (3%)
  blocking collectives  14.6 us (2%)
  between operations  13.7 us (2%)
  other arithmetic  11.6 us (2%)
    all_gather x1, waiting for transfers between devices, shards(): key_piece = lax.all_gather(keys, 'seq', axis=0, tiled=True)  126 us
    all_gather x1, waiting for transfers between devices, shards(): value_piece = lax.all_gather(values, 'seq', axis=0, tiled=True)  113 us
    all_gather x1, waiting for transfers between devices, shards(): lax.all_gather(attended, 'exp', axis=1, tiled=True)  79.5 us
    reduce_scatter x1, waiting for transfers between devices, shards(): lax.psum_scatter(spread.astype(jnp.bfloat16), 'exp', scatter_dimension=1,...  70.4 us
    reduce_scatter x1, waiting for transfers between devices, shards(): lax.psum_scatter(jnp.dot(inner_act, w_down[0], preferred_element_type=jnp...  66.4 us
    all_gather x1, waiting for transfers between devices, shards(): piece = lax.all_gather(expert_rows, 'seq', axis=0, tiled=True)  49.2 us
    while x4, local copies, waits for them, and re-layouts, shards(): lax.scan(scan_step, state, (jnp.arange(blocks, dtype=jnp.int32), key_stac...  25.5 us
    another operation x1, loops' own time, shards(): lax.scan(scan_step, state, (jnp.arange(blocks, dtype=jnp.int32), key_stac...  20.7 us
  transfers between devices with their start and end apart: 6, of which 6 were waited for; matrix products, arithmetic and copies ran while one was open for 2% of the time, Pallas kernels for 0%

commit v1 on v0

v1 whole, which is shorter than its diff:
```python
import functools
import math

import jax
import jax.numpy as jnp
from jax import lax
from jax.experimental import pallas as pl
from jax.experimental.pallas import tpu as pltpu
from jax.sharding import PartitionSpec as P

D = 8192
HD = 128


block_rows = 512


MESH = pl.DeviceIdType.MESH


def greet(peers):
    barrier = pltpu.get_barrier_semaphore()
    for peer in peers:
        pl.semaphore_signal(barrier, inc=1, device_id=peer, device_id_type=MESH)
    pl.semaphore_wait(barrier, len(peers))


def cut(start, size):
    return pl.ds(pl.multiple_of(start, size), size)


def heads_out_kernel(n, width, q_ref, k_ref, v_ref, qo, ko, vo, send, recv, own):
    me = lax.axis_index("seq")
    tokens = q_ref.shape[0]
    greet([{"seq": lax.rem(me + i, n)} for i in range(1, n)])
    pairs = ((k_ref, ko), (v_ref, vo), (q_ref, qo))
    copies = []
    for i in range(1, n):
        to = lax.rem(me + i, n)
        for t, (src, dst) in enumerate(pairs):
            copies.append(
                pltpu.make_async_remote_copy(
                    src_ref=src.at[:, cut(to * width, width)],
                    dst_ref=dst.at[cut(me * tokens, tokens), :],
                    send_sem=send.at[t * n + i],
                    recv_sem=recv.at[t * n + i],
                    device_id={"seq": to},
                    device_id_type=MESH,
                )
            )
            copies[-1].start()
    for t, (src, dst) in enumerate(pairs):
        copies.append(
            pltpu.make_async_copy(
                src.at[:, cut(me * width, width)], dst.at[cut(me * tokens, tokens), :], own.at[t]
            )
        )
        copies[-1].start()
    for copy in copies:
        copy.wait()


def heads_out(queries, keys, values, n):
    tokens, columns = queries.shape
    width = columns // n
    whole = jax.ShapeDtypeStruct((n * tokens, width), queries.dtype)
    anywhere = pl.BlockSpec(memory_space=pl.ANY)
    return pl.pallas_call(
        functools.partial(heads_out_kernel, n, width),
        out_shape=(whole, whole, whole),
        in_specs=[anywhere] * 3,
        out_specs=(anywhere,) * 3,
        scratch_shapes=[
            pltpu.SemaphoreType.DMA((3 * n,)),
            pltpu.SemaphoreType.DMA((3 * n,)),
            pltpu.SemaphoreType.DMA((3,)),
        ],
        compiler_params=pltpu.CompilerParams(collective_id=0, has_side_effects=True),
    )(queries, keys, values)


def heads_back_kernel(n, ny, width, a_ref, o_ref, s_send, s_recv, y_send, y_recv, c_send, c_recv, own):
    me = lax.axis_index("seq")
    place = lax.axis_index("exp")
    y, core = place // 2, lax.rem(place, 2)
    sibling = {"exp": y * 2 + 1 - core}
    across = [{"exp": lax.rem(y + k, ny) * 2 + core} for k in range(1, ny)]
    tokens = o_ref.shape[0]
    span = n * width
    greet([{"seq": lax.rem(me + i, n)} for i in range(1, n)] + across + [sibling])

    def piece(exp_at, seq_at):
        return o_ref.at[:, cut(exp_at * span + seq_at * width, width)]

    def push(src, dst, send, recv, peer):
        copy = pltpu.make_async_remote_copy(
            src_ref=src, dst_ref=dst, send_sem=send, recv_sem=recv, device_id=peer, device_id_type=MESH
        )
        copy.start()
        return copy

    local = pltpu.make_async_copy(a_ref.at[cut(me * tokens, tokens), :], piece(place, me), own)
    local.start()
    first = []
    for i in range(1, n):
        to = lax.rem(me + i, n)
        first.append(
            push(
                a_ref.at[cut(to * tokens, tokens), :],
                piece(place, me),
                s_send.at[i],
                s_recv.at[i],
                {"seq": to},
            )
        )
    second = []
    third = []
    for i in range(n):
        if i == 0:
            local.wait()
        else:
            first[i - 1].wait_recv()
        part = piece(place, lax.rem(me + n - i, n))
        for k in range(1, ny):
            at = i * ny + k
            second.append(push(part, part, y_send.at[at], y_recv.at[at], across[k - 1]))
        third.append(push(part, part, c_send.at[i * ny], c_recv.at[i * ny], sibling))
    for i in range(n):
        for k in range(1, ny):
            second[i * (ny - 1) + k - 1].wait_recv()
            at = i * ny + k
            part = piece(lax.rem(y + ny - k, ny) * 2 + core, lax.rem(me + n - i, n))
            third.append(push(part, part, c_send.at[at], c_recv.at[at], sibling))
    for copy in third:
        copy.wait_recv()
    for copy in first + second + third:
        copy.wait_send()


def heads_back(attended, n, n_exp):
    rows, width = attended.shape
    ny = n_exp // 2
    anywhere = pl.BlockSpec(memory_space=pl.ANY)
    return pl.pallas_call(
        functools.partial(heads_back_kernel, n, ny, width),
        out_shape=jax.ShapeDtypeStruct((rows // n, n_exp * n * width), attended.dtype),
        in_specs=[anywhere],
        out_specs=anywhere,
        scratch_shapes=[
            pltpu.SemaphoreType.DMA((n,)),
            pltpu.SemaphoreType.DMA((n,)),
            pltpu.SemaphoreType.DMA((n * ny,)),
            pltpu.SemaphoreType.DMA((n * ny,)),
            pltpu.SemaphoreType.DMA((n * ny,)),
            pltpu.SemaphoreType.DMA((n * ny,)),
            pltpu.SemaphoreType.DMA(()),
        ],
        compiler_params=pltpu.CompilerParams(collective_id=1, has_side_effects=True),
    )(attended)


def flash_kernel(block, border_ref, q_ref, k_ref, v_ref, o_ref):
    at = pl.program_id(1)
    border = border_ref[0]
    q_start = at * block
    rows = q_start + lax.broadcasted_iota(jnp.int32, (block, 1), 0)
    low = jnp.where(rows >= border, border, 0)
    steps = lax.broadcasted_iota(jnp.int32, (block, block), 1)
    q = q_ref[...]
    scale = math.log2(math.e) / math.sqrt(HD)

    def scored(j):
        start = pl.multiple_of(j * block, block)
        s = lax.dot_general(
            q, k_ref[pl.ds(start, block), :], (((1,), (1,)), ((), ())), preferred_element_type=jnp.float32
        )
        return s * scale, start

    def mix(p, start):
        return jnp.dot(
            p.astype(jnp.bfloat16), v_ref[pl.ds(start, block), :], preferred_element_type=jnp.float32
        )

    s, start = scored(at)
    s = jnp.where((steps >= low - start) & (steps <= rows - start), s, -jnp.inf)
    top = jnp.max(s, axis=1, keepdims=True)
    p = jnp.exp2(s - top)
    state = (top, jnp.sum(p, axis=1, keepdims=True), mix(p, start))

    def step(j, state):
        top, total, out = state
        s, start = scored(j)
        s = jnp.where(steps >= low - start, s, -jnp.inf)
        new_top = jnp.maximum(top, jnp.max(s, axis=1, keepdims=True))
        factor = jnp.exp2(top - new_top)
        p = jnp.exp2(s - new_top)
        return (
            new_top,
            total * factor + jnp.sum(p, axis=1, keepdims=True),
            out * factor + mix(p, start),
        )

    begin = jnp.where(q_start >= border, border // block, 0)
    top, total, out = lax.fori_loop(begin, at, step, state)
    o_ref[...] = (out / total).astype(o_ref.dtype)


def flash(queries, keys, values, border):
    rows, width = queries.shape
    block = block_rows
    return pl.pallas_call(
        functools.partial(flash_kernel, block),
        out_shape=jax.ShapeDtypeStruct((rows, width), queries.dtype),
        grid_spec=pltpu.PrefetchScalarGridSpec(
            num_scalar_prefetch=1,
            grid=(width // HD, rows // block),
            in_specs=[
                pl.BlockSpec((block, HD), lambda h, i, b: (i, h)),
                pl.BlockSpec((rows, HD), lambda h, i, b: (0, h)),
                pl.BlockSpec((rows, HD), lambda h, i, b: (0, h)),
            ],
            out_specs=pl.BlockSpec((block, HD), lambda h, i, b: (i, h)),
        ),
    )(border, queries, keys, values)


def attend_by_head(queries, keys, values, documents, n, n_exp):
    border = jnp.sum((documents == 0).astype(jnp.int32)).reshape(1)
    q_all, k_all, v_all = heads_out(queries, keys, values, n)
    return heads_back(flash(q_all, k_all, v_all, border), n, n_exp)


def attend_by_token(queries, keys, values, documents):
    tokens = queries.shape[0]
    heads_here = queries.shape[1] // HD
    seq_pos = lax.axis_index("seq")
    start_row = seq_pos * tokens
    query_pos = start_row + jnp.arange(tokens, dtype=jnp.int32)
    query_doc = lax.dynamic_slice_in_dim(documents, start_row, tokens, 0)
    query_heads = queries.reshape(tokens, heads_here, HD)
    score_scale = 1.0 / math.sqrt(HD)

    def attend(state, key_rows, value_rows, key_start):
        row_count = key_rows.shape[0]
        key_pos = key_start + jnp.arange(row_count, dtype=jnp.int32)
        key_doc = lax.dynamic_slice_in_dim(documents, key_start, row_count, 0)
        scores = (
            jnp.einsum(
                "qhd,khd->qhk",
                query_heads,
                key_rows.reshape(row_count, heads_here, HD),
                preferred_element_type=jnp.float32,
            )
            * score_scale
        )
        allowed = (key_pos[None, :] <= query_pos[:, None]) & (
            key_doc[None, :] == query_doc[:, None]
        )
        scores = jnp.where(allowed[:, None, :], scores, -jnp.inf)
        running_max, running_sum, running_out = state
        new_max = jnp.maximum(running_max, jnp.max(scores, axis=2))
        factor = jnp.exp(running_max - new_max)
        weights = jnp.exp(scores - new_max[:, :, None])
        running_sum = running_sum * factor + jnp.sum(weights, axis=2)
        running_out = running_out * factor[:, :, None] + jnp.einsum(
            "qhk,khd->qhd",
            weights.astype(jnp.bfloat16),
            value_rows.reshape(row_count, heads_here, HD),
            preferred_element_type=jnp.float32,
        )
        return (new_max, running_sum, running_out)

    def visit_block(state, key_rows, value_rows, key_start):
        row_count = key_rows.shape[0]
        last_doc = lax.dynamic_index_in_dim(documents, key_start + row_count - 1, 0, keepdims=False)
        beyond = (key_start > query_pos[tokens - 1]) | (last_doc < query_doc[0])
        return lax.cond(
            beyond,
            lambda inner_state: inner_state,
            lambda inner_state: attend(inner_state, key_rows, value_rows, key_start),
            state,
        )

    initial = (
        jnp.full((tokens, heads_here), -1e30, jnp.float32),
        jnp.zeros((tokens, heads_here), jnp.float32),
        jnp.zeros((tokens, heads_here, HD), jnp.float32),
    )
    state = initial
    key_piece = lax.all_gather(keys, "seq", axis=0, tiled=True)
    value_piece = lax.all_gather(values, "seq", axis=0, tiled=True)
    row_count = key_piece.shape[0]
    blocks = row_count // block_rows
    key_stack = key_piece.reshape(blocks, block_rows, key_piece.shape[1])
    value_stack = value_piece.reshape(blocks, block_rows, value_piece.shape[1])

    def scan_step(inner_state, block_item):
        block_index, key_rows, value_rows = block_item
        return (visit_block(inner_state, key_rows, value_rows, block_index * block_rows), None)

    state, unused = lax.scan(
        scan_step, state, (jnp.arange(blocks, dtype=jnp.int32), key_stack, value_stack)
    )
    running_max, running_sum, running_out = state
    attended = (
        (running_out / running_sum[:, :, None])
        .reshape(tokens, heads_here * HD)
        .astype(jnp.bfloat16)
    )
    return lax.all_gather(attended, "exp", axis=1, tiled=True)


def shards(
    residual,
    queries,
    keys,
    values,
    documents,
    out_proj,
    modality,
    norm_gain,
    picks,
    router,
    w_gate,
    w_up,
    w_down,
):
    tokens = queries.shape[0]
    seq_pos = lax.axis_index("seq")
    start_row = seq_pos * tokens
    n_seq, n_exp = lax.axis_size("seq"), lax.axis_size("exp")
    if (queries.shape[1] // HD) % n_seq == 0 and n_exp % 2 == 0:
        attended = attend_by_head(queries, keys, values, documents, n_seq, n_exp)
    else:
        attended = attend_by_token(queries, keys, values, documents)
    mixed = jnp.dot(
        attended,
        out_proj,
        preferred_element_type=jnp.float32,
    )
    hidden_state = (residual.astype(jnp.float32) + mixed).astype(jnp.bfloat16)
    hidden_wide = hidden_state.astype(jnp.float32)
    square_total = lax.psum(jnp.sum(hidden_wide * hidden_wide, axis=1), "exp")
    inverse = lax.rsqrt(square_total / D + 1e-05)
    gain_rows = jnp.where(modality[:, None] == 0, norm_gain[0][None, :], norm_gain[1][None, :])
    normed = (hidden_wide * inverse[:, None] * gain_rows).astype(jnp.bfloat16)
    capacity = tokens // 32
    inside = (picks >= start_row) & (picks < start_row + tokens)
    slot_index = jnp.cumsum(inside.astype(jnp.int32), axis=1) - 1
    matched = inside[:, None, :] & (
        slot_index[:, None, :] == jnp.arange(capacity, dtype=jnp.int32)[None, :, None]
    )
    local_index = jnp.sum(jnp.where(matched, picks[:, None, :] - start_row, 0), axis=2)
    filled = jnp.any(matched, axis=2)
    rows_out = jnp.take(normed, local_index.T, axis=0)
    rows_out = jnp.where(filled.T[:, :, None], rows_out, jnp.zeros_like(rows_out))
    arrived = lax.all_to_all(rows_out, "exp", split_axis=1, concat_axis=1, tiled=True)
    expert_rows = arrived.reshape(capacity, D)
    logits = jnp.dot(expert_rows, router, preferred_element_type=jnp.float32)[:, 0]
    piece = lax.all_gather(expert_rows, "seq", axis=0, tiled=True)
    gate_part = jnp.dot(piece, w_gate[0], preferred_element_type=jnp.float32)
    up_part = jnp.dot(piece, w_up[0], preferred_element_type=jnp.float32)
    inner_act = (jax.nn.silu(gate_part) * up_part).astype(jnp.bfloat16)
    summed = lax.psum_scatter(
        jnp.dot(inner_act, w_down[0], preferred_element_type=jnp.float32).astype(jnp.bfloat16),
        "seq",
        scatter_dimension=0,
        tiled=True,
    ).astype(jnp.float32)
    weighted = (jax.nn.sigmoid(logits)[:, None] * summed).astype(jnp.bfloat16)
    sliced = weighted.reshape(capacity, n_exp, D // n_exp)
    returned = lax.all_to_all(sliced, "exp", split_axis=1, concat_axis=0, tiled=True)
    returned = returned.reshape(n_exp * capacity, D // n_exp)
    placing = (
        (jnp.arange(tokens, dtype=jnp.int32)[:, None] == local_index.reshape(1, -1))
        & filled.reshape(1, -1)
    ).astype(jnp.bfloat16)
    expert_add = jnp.dot(placing, returned, preferred_element_type=jnp.float32)
    return (hidden_wide + expert_add).astype(jnp.bfloat16)


def solution(mesh):
    return jax.shard_map(
        shards,
        mesh=mesh,
        in_specs=(
            P("seq", "exp"),
            P("seq", "exp"),
            P("seq", "exp"),
            P("seq", "exp"),
            P(),
            P(None, "exp"),
            P("seq"),
            P(None, "exp"),
            P(),
            P(None, "exp"),
            P("exp", None, "seq"),
            P("exp", None, "seq"),
            P("exp", "seq", None),
        ),
        out_specs=P("seq", "exp"),
        check_vma=False,
    )
```

time: 665 us -> 335 us (0.50)
  waiting for transfers between devices: 506 us -> 125 us
  Pallas kernels: 0 us -> 133 us
  local copies, waits for them, and re-layouts: 59.3 us -> 5.57 us
  loops' own time: 20.9 us -> 0 us
  matrix products: 41 us -> 31.4 us
    all_gather x3 -> x0, waiting for transfers between devices: 318 us -> none  [the longest x1 126 us: shards(): key_piece = lax.all_gather(keys, 'seq', axis=0, tiled=True)]
    pallas_call x0 -> x3, Pallas kernels: none -> 133 us  [the longest x1 57.4 us: heads_out(): pl.pallas_call(functools.partial(heads_out_kernel, n, width), out_shape=(...]
    reduce_scatter x1 -> x0, waiting for transfers between devices: 70.4 us -> none  [shards(): lax.psum_scatter(spread.astype(jnp.bfloat16), 'exp', scatter_dimension=1,...]
    while x12 -> x0, local copies, waits for them, and re-layouts: 25.5 us -> none  [the longest x4 25.5 us: shards(): lax.scan(scan_step, state, (jnp.arange(blocks, dtype=jnp.int32), key_stac...]
    another operation x9 -> x0, loops' own time: 20.9 us -> none  [the longest x1 20.7 us: shards(): lax.scan(scan_step, state, (jnp.arange(blocks, dtype=jnp.int32), key_stac...]
    dynamic_slice x19 -> x0, local copies, waits for them, and re-layouts: 18.7 us -> none  [the longest x8 10.4 us: visit_block(): lax.dynamic_index_in_dim(documents, key_start + row_count - 1, 0, keepdim...]
    dot_general x4 -> x2, matrix products: 25.8 us -> 16.2 us  [the longest x1 14.2 us: shards(): mixed = jnp.dot(attended, out_proj, preferred_element_type=jnp.float32)]
    slice x16 -> x0, local copies, waits for them, and re-layouts: 9.43 us -> none  [visit_block(): beyond = (key_start > query_pos[tokens - 1]) | (last_doc < query_doc[0])]
  transfers between devices with their start and end apart: 6 -> 3, of which waited for: 6 -> 3; matrix products, arithmetic and copies ran while one was open for 2% -> 0% of each run, Pallas kernels for 0% -> 0%
where the time goes in v1:
time: 335 us
  Pallas kernels  133 us (40%)
  waiting for transfers between devices  125 us (37%)
  matrix products  31.4 us (9%)
  blocking collectives  14.8 us (4%)
  between operations  13.5 us (4%)
  other arithmetic  7.51 us (2%)
  local copies, waits for them, and re-layouts  5.57 us (2%)
  starting transfers between devices  3.63 us (1%)
    reduce_scatter x1, waiting for transfers between devices, shards(): lax.psum_scatter(jnp.dot(inner_act, w_down[0], preferred_element_type=jnp...  67.3 us
    pallas_call x1, Pallas kernels, heads_out(): pl.pallas_call(functools.partial(heads_out_kernel, n, width), out_shape=(...  57.4 us
    pallas_call x1, Pallas kernels, heads_back(): pl.pallas_call(functools.partial(heads_back_kernel, n, ny, width), out_sh...  53.4 us
    all_gather x1, waiting for transfers between devices, shards(): piece = lax.all_gather(expert_rows, 'seq', axis=0, tiled=True)  51.9 us
    pallas_call x1, Pallas kernels, flash(): pl.pallas_call(functools.partial(flash_kernel, block), out_shape=jax.Shap...  22.5 us
    dot_general x1, matrix products, shards(): mixed = jnp.dot(attended, out_proj, preferred_element_type=jnp.float32)  14.2 us
    dot_general x1, matrix products, shards(): jnp.dot(inner_act, w_down[0], preferred_element_type=jnp.float32)  9.64 us
    all_to_all x1, blocking collectives, shards(): lax.all_to_all(rows_out, 'exp', split_axis=1, concat_axis=1, tiled=True)  8.7 us
  transfers between devices with their start and end apart: 3, of which 3 were waited for; matrix products, arithmetic and copies ran while one was open for 0% of the time, Pallas kernels for 0%

profile of v1, /device:TPU:0, one launch (start us, length us, event | category | flops | bytes accessed | tf_op | source)
XLA Modules:
  0.0 334.8 jit_solution(15937571731112288447)
XLA Ops:
  6.5 0.7 fusion.35
  7.2 0.2 reduce_window_sum.11
  7.5 0.7 broadcast_add_fusion
  8.2 0.1 fusion.33
  8.3 0.2 select_reduce_fusion
  8.5 1.3 convert_reduce_fusion
  9.8 0.7 broadcast_compare_fusion
  10.6 0.1 reshape.54
  10.7 0.8 fusion.36
  11.5 57.4 %shard_map.127 = (bf16[4096,128]{1,0:T(8,128)(2,1)}, bf16[4096,128]{1,0:T(8,128)(2,1)}, bf16[4096,128]{1,0:T(8,128)(2,1)}) custom-call(bf16[512,1024]{1,0:T(8,128)(2,1)} %q_ref.1, bf16[512,1024]{1,0:T(8,128)(2,1)} %k_ref.1, bf16[512,1024]{1,0:T(8,128)(2,1)} %v_ref.1), custom_call_target="tpu_custom_call" | custom-call | tf_op jit(solution)/shard_map/pallas_call | solution.py:68
  68.9 22.5 %shard_map.128.a_ref = bf16[4096,128]{1,0:T(8,128)(2,1)} custom-call(s32[1]{0:T(128)} %bitcast.border_ref, bf16[4096,128]{1,0:T(8,128)(2,1)} %get-tuple-element.8.q_ref, bf16[4096,128]{1,0:T(8,128)(2,1)} %get-tuple-element.9.k_ref, bf16[4096,128]{1,0:T(8,128)(2,1)} %get-tuple-element.10.v_ref), custom_call_target="tpu_custom_call" | custom-call | tf_op jit(solution)/shard_map/pallas_call | solution.py:211
  91.4 53.4 %shard_map.129 = bf16[512,4096]{1,0:T(8,128)(2,1)} custom-call(bf16[4096,128]{1,0:T(8,128)(2,1)} %shard_map.128.a_ref), custom_call_target="tpu_custom_call" | custom-call | tf_op jit(solution)/shard_map/pallas_call | solution.py:144
  144.9 14.2 %fusion.5 = (f32[512]{0:T(512)S(1)}, bf16[512,2048]{1,0:T(8,128)(2,1)S(1)}) fusion(bf16[512,4096]{1,0:T(8,128)(2,1)} %shard_map.129, bf16[4096,2048]{1,0:T(8,128)(2,1)} %param.18, bf16[512,2048]{1,0:T(8,128)(2,1)} %param.13), kind=kOutput, calls=%fused_computation.10 | convolution fusion | flops 8596226048 | bytes 25167872 | tf_op jit(solution)/shard_map/dot_general | solution.py:336
  159.1 6.1 %psum.7 = f32[512]{0:T(512)S(1)} all-reduce(f32[512]{0:T(512)S(1)} %get-tuple-element.15), channel_id=1, replica_groups=mesh['seq'=8,'exp'=4] {'exp'}, use_global_device_ids=true, to_apply=%region_5.6 | all-reduce | flops 512 | bytes 4096 | tf_op jit(solution)/shard_map/psum | solution.py:343
  165.1 2.2 fusion.7
  167.3 2.8 gather_fusion
  170.1 0.1 reshape.53
  170.3 0.3 fusion.21
  170.6 8.7 %all_to_all.20 = bf16[16,4,2048]{2,0,1:T(8,128)(2,1)S(1)} all-to-all(bf16[16,4,2048]{2,0,1:T(8,128)(2,1)S(1)} %fusion.21), channel_id=1, replica_groups=mesh['seq'=8,'exp'=4] {'exp'}, dimensions={1} | all-to-all | bytes 524288 | tf_op jit(solution)/shard_map/all_to_all | solution.py:357
  179.3 0.7 copy.33
  180.1 0.2 reduce-scatter.2.cloned.1.call-start
  180.3 51.9 %all-gather.2.cloned.1.call-done = bf16[128,8192]{1,0:T(8,128)(2,1)} async-done(((bf16[16,8192]{1,0:T(8,128)(2,1)}), bf16[128,8192]{1,0:T(8,128)(2,1)}) %all-gather.2.cloned.1.call-update) | async-done | bytes 2097168 | tf_op jit(solution)/shard_map/all_gather | solution.py:360
  232.2 5.4 %fusion.3 = f32[128,512]{1,0:T(8,128)S(1)} fusion(bf16[128,8192]{1,0:T(8,128)(2,1)} %all-gather.2.cloned.1.call-done, bf16[1,8192,512]{2,1,0:T(8,128)(2,1)} %param.23), kind=kOutput, calls=%fused_computation.5 | convolution fusion | flops 1073741824 | bytes 10747904 | tf_op jit(solution)/shard_map/dot_general | solution.py:361
  237.6 9.6 %convolution_convert_fusion = bf16[128,8192]{1,0:T(8,128)(2,1)} fusion(bf16[1,512,8192]{2,1,0:T(8,128)(2,1)} %param.25, bf16[128,8192]{1,0:T(8,128)(2,1)S(1)} %copy-done.1, bf16[1,8192,512]{2,1,0:T(8,128)(2,1)} %param.24, f32[128,512]{1,0:T(8,128)S(1)} %fusion.3), kind=kOutput, calls=%fused_computation.1 | convolution fusion | flops 2148925440 | bytes 21233664 | tf_op jit(solution)/shard_map/dot_general | solution.py:365
  247.3 0.2 fusion.18
  247.5 67.3 %reduce-scatter.2.cloned.1.call-done = bf16[16,8192]{1,0:T(8,128)(2,1)} async-done(((bf16[128,8192]{1,0:T(8,128)(2,1)}), bf16[16,8192]{1,0:T(8,128)(2,1)}) %reduce-scatter.2.cloned.1.call-update) | async-done | bytes 262160 | tf_op jit(solution)/shard_map/reduce_scatter | solution.py:364
  314.8 1.1 multiply_convert_fusion
  315.9 0.7 copy.38
  316.6 3.4 %all-to-all-start.1 = ((bf16[16,4,2048]{2,0,1:T(8,128)(2,1)}), bf16[16,4,2048]{2,0,1:T(8,128)(2,1)S(1)}, u32[]{:S(2)}, u32[]{:S(2)}) async-start(bf16[16,4,2048]{2,0,1:T(8,128)(2,1)} %bitcast.50), calls=%async_computation.2 | async-start | bytes 524288 | tf_op jit(solution)/shard_map/all_to_all | solution.py:372
  320.0 0.1 and.30
  320.2 5.8 %all-to-all-done.1 = bf16[16,4,2048]{2,0,1:T(8,128)(2,1)S(1)} async-done(((bf16[16,4,2048]{2,0,1:T(8,128)(2,1)}), bf16[16,4,2048]{2,0,1:T(8,128)(2,1)S(1)}, u32[]{:S(2)}, u32[]{:S(2)}) %all-to-all-start.1) | async-done | bytes 262176 | tf_op jit(solution)/shard_map/all_to_all | solution.py:372
  326.0 2.0 fusion.8
  (19 shorter events, 0.3 us)
Async XLA Ops:
  6.5 240.7 %copy-start = (bf16[8192,1]{0,1:T(2,128)(2,1)S(1)}, bf16[8192,1]{0,1:T(2,128)(2,1)}, u32[]{:S(2)}) copy-start(bf16[8192,1]{0,1:T(2,128)(2,1)} %param.22) | copy-start | bytes 49156
  6.5 225.6 %all-gather.2.cloned.1.call-start = ((), (), s32[]{:S(2)}) async-start(), calls=%async_computation.3 | async-start | bytes 2359296 | tf_op jit(solution)/shard_map/all_gather | solution.py:360
  159.0 21.0 %copy-start.2 = (bf16[512,2048]{1,0:T(8,128)(2,1)}, bf16[512,2048]{1,0:T(8,128)(2,1)S(1)}, u32[]{:S(2)}) copy-start(bf16[512,2048]{1,0:T(8,128)(2,1)S(1)} %get-tuple-element.16) | copy-start | bytes 6291460
  180.1 134.7 %reduce-scatter.2.cloned.1.call-start = ((), (), s32[]{:S(2)}) async-start(), calls=%async_computation.4 | async-start | bytes 2359296 | tf_op jit(solution)/shard_map/reduce_scatter | solution.py:364
  232.2 5.4 %copy-start.1 = (bf16[128,8192]{1,0:T(8,128)(2,1)S(1)}, bf16[128,8192]{1,0:T(8,128)(2,1)}, u32[]{:S(2)}) copy-start(bf16[128,8192]{1,0:T(8,128)(2,1)} %all-gather.2.cloned.1.call-done) | copy-start | bytes 6291460
  237.6 9.7 %copy-start.4 = (bf16[4,2,8,2048]{3,2,0,1:T(8,128)(2,1)S(1)}, bf16[4,2,8,2048]{3,2,0,1:T(8,128)(2,1)}, u32[]{:S(2)}) copy-start(bf16[4,2,8,2048]{3,2,0,1:T(8,128)(2,1)} %copy.33) | copy-start | bytes 786436
  247.3 78.7 %copy-start.3 = (bf16[512,2048]{1,0:T(8,128)(2,1)S(1)}, bf16[512,2048]{1,0:T(8,128)(2,1)}, u32[]{:S(2)}) copy-start(bf16[512,2048]{1,0:T(8,128)(2,1)} %copy-done.2) | copy-start | bytes 6291460
  316.6 9.4 %all-to-all-start.1 = ((bf16[16,4,2048]{2,0,1:T(8,128)(2,1)}), bf16[16,4,2048]{2,0,1:T(8,128)(2,1)S(1)}, u32[]{:S(2)}, u32[]{:S(2)}) async-start(bf16[16,4,2048]{2,0,1:T(8,128)(2,1)} %bitcast.50), calls=%async_computation.2 | async-start | bytes 524288 | tf_op jit(solution)/shard_map/all_to_all | solution.py:372
Sparse Core Ops, SparseCore 0:
  180.2 51.9 all-gather.1
  247.4 67.3 reduce-scatter.1

commit v2 on v1

--- a/solution.py
+++ b/solution.py
@@ -92,13 +92,6 @@
     def piece(exp_at, seq_at):
         return o_ref.at[:, cut(exp_at * span + seq_at * width, width)]
 
-    def push(src, dst, send, recv, peer):
-        copy = pltpu.make_async_remote_copy(
-            src_ref=src, dst_ref=dst, send_sem=send, recv_sem=recv, device_id=peer, device_id_type=MESH
-        )
-        copy.start()
-        return copy
-
     local = pltpu.make_async_copy(a_ref.at[cut(me * tokens, tokens), :], piece(place, me), own)
     local.start()
     first = []
@@ -157,6 +150,118 @@
         ],
         compiler_params=pltpu.CompilerParams(collective_id=1, has_side_effects=True),
     )(attended)
+
+
+def push(src, dst, send, recv, peer):
+    copy = pltpu.make_async_remote_copy(
+        src_ref=src, dst_ref=dst, send_sem=send, recv_sem=recv, device_id=peer, device_id_type=MESH
+    )
+    copy.start()
+    return copy
+
+
+def lines(me, nz):
+    z, x = me // 2, lax.rem(me, 2)
+    along = [{"seq": lax.rem(z + k, nz) * 2 + x} for k in range(1, nz)]
+    return z, x, along, {"seq": z * 2 + 1 - x}
+
+
+def rows_kernel(nz, ne, cap, width, r_ref, o_ref, e_send, e_recv, z_send, z_recv, x_send, x_recv, own):
+    me = lax.axis_index("seq")
+    place = lax.axis_index("exp")
+    z, x, along, partner = lines(me, nz)
+    others = [{"exp": lax.rem(place + i, ne)} for i in range(1, ne)]
+    greet(others + along + [partner])
+
+    def piece(z_at, exp_at):
+        return o_ref.at[cut((z_at * 2 + x) * cap, cap), cut(exp_at * width, width)]
+
+    local = pltpu.make_async_copy(r_ref.at[cut(place * cap, cap), :], piece(z, place), own)
+    local.start()
+    first = []
+    for i in range(1, ne):
+        src = r_ref.at[cut(lax.rem(place + i, ne) * cap, cap), :]
+        first.append(push(src, piece(z, place), e_send.at[i], e_recv.at[i], others[i - 1]))
+    second = []
+    third = []
+    for i in range(ne):
+        if i == 0:
+            local.wait()
+        else:
+            first[i - 1].wait_recv()
+        part = piece(z, lax.rem(place + ne - i, ne))
+        for k in range(1, nz):
+            at = i * nz + k
+            second.append(push(part, part, z_send.at[at], z_recv.at[at], along[k - 1]))
+        third.append(push(part, part, x_send.at[i * nz], x_recv.at[i * nz], partner))
+    for k in range(1, nz):
+        for i in range(ne):
+            second[i * (nz - 1) + k - 1].wait_recv()
+            at = i * nz + k
+            part = piece(lax.rem(z + nz - k, nz), lax.rem(place + ne - i, ne))
+            third.append(push(part, part, x_send.at[at], x_recv.at[at], partner))
+    for copy in third:
+        copy.wait_recv()
+    for copy in first + second + third:
+        copy.wait_send()
+
+
+def share_rows(rows, n, ne):
+    cap, width = rows.shape[0] // ne, rows.shape[1]
+    nz = n // 2
+    anywhere = pl.BlockSpec(memory_space=pl.ANY)
+    return pl.pallas_call(
+        functools.partial(rows_kernel, nz, ne, cap, width),
+        out_shape=jax.ShapeDtypeStruct((n * cap, ne * width), rows.dtype),
+        in_specs=[anywhere],
+        out_specs=anywhere,
+        scratch_shapes=[pltpu.SemaphoreType.DMA((ne,))] * 2
+        + [pltpu.SemaphoreType.DMA((ne * nz,))] * 4
+        + [pltpu.SemaphoreType.DMA(())],
+        compiler_params=pltpu.CompilerParams(collective_id=2, has_side_effects=True),
+    )(rows)
+
+
+def sums_kernel(nz, cap, p_ref, o_ref, x_buf, s_buf, z_buf, x_send, x_recv, z_send, z_recv):
+    me = lax.axis_index("seq")
+    z, x, along, partner = lines(me, nz)
+    greet(along + [partner])
+
+    def rows_of(k, side):
+        return cut((lax.rem(z + k, nz) * 2 + side) * cap, cap)
+
+    order = list(range(1, nz)) + [0]
+    pairs = {}
+    for k in order:
+        pairs[k] = push(p_ref.at[rows_of(k, 1 - x), :], x_buf.at[k], x_send.at[k], x_recv.at[k], partner)
+    sent = []
+    for k in order:
+        pairs[k].wait_recv()
+        both = p_ref[rows_of(k, x), :].astype(jnp.float32) + x_buf[k].astype(jnp.float32)
+        if k:
+            s_buf[k] = both.astype(jnp.bfloat16)
+            sent.append(push(s_buf.at[k], z_buf.at[k], z_send.at[k], z_recv.at[k], along[k - 1]))
+        else:
+            o_ref[...] = both
+    for k in range(1, nz):
+        sent[k - 1].wait_recv()
+        o_ref[...] += z_buf[k].astype(jnp.float32)
+    for copy in list(pairs.values()) + sent:
+        copy.wait_send()
+
+
+def sum_rows(partial, n):
+    cap, width = partial.shape[0] // n, partial.shape[1]
+    nz = n // 2
+    slots = pltpu.VMEM((nz, cap, width), jnp.bfloat16)
+    return pl.pallas_call(
+        functools.partial(sums_kernel, nz, cap),
+        out_shape=jax.ShapeDtypeStruct((cap, width), jnp.float32),
+        in_specs=[pl.BlockSpec(memory_space=pltpu.VMEM)],
+        out_specs=pl.BlockSpec(memory_space=pltpu.VMEM),
+        scratch_shapes=[slots, slots, slots] + [pltpu.SemaphoreType.DMA((nz,))] * 4,
+        compiler_params=pltpu.CompilerParams(collective_id=3, has_side_effects=True),
+    )(partial)
 
 
 def flash_kernel(block, border_ref, q_ref, k_ref, v_ref, o_ref):
@@ -352,21 +457,17 @@
     )
     local_index = jnp.sum(jnp.where(matched, picks[:, None, :] - start_row, 0), axis=2)
     filled = jnp.any(matched, axis=2)
-    rows_out = jnp.take(normed, local_index.T, axis=0)
-    rows_out = jnp.where(filled.T[:, :, None], rows_out, jnp.zeros_like(rows_out))
-    arrived = lax.all_to_all(rows_out, "exp", split_axis=1, concat_axis=1, tiled=True)
-    expert_rows = arrived.reshape(capacity, D)
+    rows_out = jnp.take(normed, local_index.reshape(-1), axis=0)
+    rows_out = jnp.where(filled.reshape(-1, 1), rows_out, jnp.zeros_like(rows_out))
+    piece = share_rows(rows_out, n_seq, n_exp)
+    expert_rows = lax.dynamic_slice_in_dim(piece, seq_pos * capacity, capacity, 0)
     logits = jnp.dot(expert_rows, router, preferred_element_type=jnp.float32)[:, 0]
-    piece = lax.all_gather(expert_rows, "seq", axis=0, tiled=True)
     gate_part = jnp.dot(piece, w_gate[0], preferred_element_type=jnp.float32)
     up_part = jnp.dot(piece, w_up[0], preferred_element_type=jnp.float32)
     inner_act = (jax.nn.silu(gate_part) * up_part).astype(jnp.bfloat16)
-    summed = lax.psum_scatter(
-        jnp.dot(inner_act, w_down[0], preferred_element_type=jnp.float32).astype(jnp.bfloat16),
-        "seq",
-        scatter_dimension=0,
-        tiled=True,
-    ).astype(jnp.float32)
+    summed = sum_rows(
+        jnp.dot(inner_act, w_down[0], preferred_element_type=jnp.float32).astype(jnp.bfloat16), n_seq
+    )
     weighted = (jax.nn.sigmoid(logits)[:, None] * summed).astype(jnp.bfloat16)
     sliced = weighted.reshape(capacity, n_exp, D // n_exp)
     returned = lax.all_to_all(sliced, "exp", split_axis=1, concat_axis=0, tiled=True)

time: 335 us -> 270 us (0.81)
  waiting for transfers between devices: 125 us -> 0 us
  Pallas kernels: 133 us -> 210 us
  between operations: 13.5 us -> 0.12 us
  starting transfers between devices: 3.63 us -> 0 us
    pallas_call x0 -> x2, Pallas kernels: none -> 76.6 us  [the longest x1 40.9 us: share_rows(): pl.pallas_call(functools.partial(rows_kernel, nz, ne, cap, width), out_sh...]
    reduce_scatter x1 -> x0, waiting for transfers between devices: 67.3 us -> none  [shards(): lax.psum_scatter(jnp.dot(inner_act, w_down[0], preferred_element_type=jnp...]
    all_gather x1 -> x0, waiting for transfers between devices: 51.9 us -> none  [shards(): piece = lax.all_gather(expert_rows, 'seq', axis=0, tiled=True)]
    all_to_all x1 -> x0, waiting for transfers between devices: 5.8 us -> none  [shards(): lax.all_to_all(sliced, 'exp', split_axis=1, concat_axis=0, tiled=True)]
    all_to_all x1 -> x0, starting transfers between devices: 3.4 us -> none  [shards(): lax.all_to_all(sliced, 'exp', split_axis=1, concat_axis=0, tiled=True)]
  transfers between devices with their start and end apart: 3 -> 0, of which waited for: 3 -> 0; matrix products, arithmetic and copies ran while one was open for 0% -> 0% of each run, Pallas kernels for 0% -> 0%
where the time goes in v2:
time: 270 us
  Pallas kernels  210 us (78%)
  matrix products  33 us (12%)
  blocking collectives  14.6 us (5%)
  other arithmetic  8.12 us (3%)
  local copies, waits for them, and re-layouts  3.94 us (1%)
    pallas_call x1, Pallas kernels, heads_out(): pl.pallas_call(functools.partial(heads_out_kernel, n, width), out_shape=(...  57.4 us
    pallas_call x1, Pallas kernels, heads_back(): pl.pallas_call(functools.partial(heads_back_kernel, n, ny, width), out_sh...  53.4 us
    pallas_call x1, Pallas kernels, share_rows(): pl.pallas_call(functools.partial(rows_kernel, nz, ne, cap, width), out_sh...  40.9 us
    pallas_call x1, Pallas kernels, sum_rows(): pl.pallas_call(functools.partial(sums_kernel, nz, cap), out_shape=jax.Sha...  35.7 us
    pallas_call x1, Pallas kernels, flash(): pl.pallas_call(functools.partial(flash_kernel, block), out_shape=jax.Shap...  22.5 us
    dot_general x1, matrix products, shards(): mixed = jnp.dot(attended, out_proj, preferred_element_type=jnp.float32)  14.2 us
    dot_general x1, matrix products, shards(): jnp.dot(inner_act, w_down[0], preferred_element_type=jnp.float32)  9.61 us
    all_to_all x1, blocking collectives, shards(): lax.all_to_all(sliced, 'exp', split_axis=1, concat_axis=0, tiled=True)  8.39 us

profile of v2, /device:TPU:0, one launch (start us, length us, event | category | flops | bytes accessed | tf_op | source)
XLA Modules:
  0.0 269.8 jit_solution(13700441776847528440)
XLA Ops:
  0.0 0.0 copy-start
  0.0 0.7 fusion.37
  0.7 0.2 reduce_window_sum.11
  0.9 0.7 broadcast_add_fusion
  1.6 0.1 fusion.33
  1.8 0.2 select_reduce_fusion
  1.9 0.1 eq.47
  2.0 0.1 reshape.78
  2.1 1.3 convert_reduce_fusion
  3.4 0.7 broadcast_compare_fusion
  4.1 0.1 and.32
  4.2 0.8 fusion.38
  5.0 57.4 %shard_map.127 = (bf16[4096,128]{1,0:T(8,128)(2,1)}, bf16[4096,128]{1,0:T(8,128)(2,1)}, bf16[4096,128]{1,0:T(8,128)(2,1)}) custom-call(bf16[512,1024]{1,0:T(8,128)(2,1)} %q_ref.1, bf16[512,1024]{1,0:T(8,128)(2,1)} %k_ref.1, bf16[512,1024]{1,0:T(8,128)(2,1)} %v_ref.1), custom_call_target="tpu_custom_call" | custom-call | tf_op jit(solution)/shard_map/pallas_call | solution.py:68
  62.4 22.5 %shard_map.128.a_ref = bf16[4096,128]{1,0:T(8,128)(2,1)} custom-call(s32[1]{0:T(128)} %bitcast.border_ref, bf16[4096,128]{1,0:T(8,128)(2,1)} %get-tuple-element.8.q_ref, bf16[4096,128]{1,0:T(8,128)(2,1)} %get-tuple-element.9.k_ref, bf16[4096,128]{1,0:T(8,128)(2,1)} %get-tuple-element.10.v_ref), custom_call_target="tpu_custom_call" | custom-call | tf_op jit(solution)/shard_map/pallas_call | solution.py:316
  85.0 53.4 %shard_map.129 = bf16[512,4096]{1,0:T(8,128)(2,1)} custom-call(bf16[4096,128]{1,0:T(8,128)(2,1)} %shard_map.128.a_ref), custom_call_target="tpu_custom_call" | custom-call | tf_op jit(solution)/shard_map/pallas_call | solution.py:137
  138.4 14.2 %fusion.5 = (f32[512]{0:T(512)S(1)}, bf16[512,2048]{1,0:T(8,128)(2,1)S(1)}) fusion(bf16[512,4096]{1,0:T(8,128)(2,1)} %shard_map.129, bf16[4096,2048]{1,0:T(8,128)(2,1)} %param.18, bf16[512,2048]{1,0:T(8,128)(2,1)} %param.13), kind=kOutput, calls=%fused_computation.10 | convolution fusion | flops 8596226048 | bytes 25167872 | tf_op jit(solution)/shard_map/dot_general | solution.py:441
  152.6 0.0 copy-start.2
  152.6 6.2 %psum.7 = f32[512]{0:T(512)S(1)} all-reduce(f32[512]{0:T(512)S(1)} %get-tuple-element.15), channel_id=1, replica_groups=mesh['seq'=8,'exp'=4] {'exp'}, use_global_device_ids=true, to_apply=%region_5.6 | all-reduce | flops 512 | bytes 4096 | tf_op jit(solution)/shard_map/psum | solution.py:448
  158.8 2.2 fusion.7
  161.0 2.8 %gather_fusion = bf16[64,2048]{1,0:T(8,128)(2,1)S(1)} fusion(bf16[512,2048]{1,0:T(8,128)(2,1)} %fusion.7, s32[1024]{0:T(1024)S(1)} %pad_clamp_fusion), kind=kCustom, calls=%fused_computation | custom fusion | bytes 524544 | tf_op jit(solution)/shard_map/jit(_take)/gather | solution.py:460
  163.8 0.8 select_select_fusion.r_ref
  164.7 0.0 copy-done.2
  164.7 40.9 %shard_map.130 = bf16[128,8192]{1,0:T(8,128)(2,1)} custom-call(bf16[64,2048]{1,0:T(8,128)(2,1)} %select_select_fusion.r_ref), custom_call_target="tpu_custom_call" | custom-call | tf_op jit(solution)/shard_map/pallas_call | solution.py:213
  205.6 0.0 copy-start.1
  205.6 5.4 %fusion.3 = f32[128,512]{1,0:T(8,128)S(1)} fusion(bf16[128,8192]{1,0:T(8,128)(2,1)} %shard_map.130, bf16[1,8192,512]{2,1,0:T(8,128)(2,1)} %param.23), kind=kOutput, calls=%fused_computation.5 | convolution fusion | flops 1073741824 | bytes 10747904 | tf_op jit(solution)/shard_map/dot_general | solution.py:465
  211.0 0.0 copy-done.1
  211.0 9.6 %convolution_convert_fusion.p_ref = bf16[128,8192]{1,0:T(8,128)(2,1)} fusion(bf16[1,512,8192]{2,1,0:T(8,128)(2,1)} %param.25, bf16[128,8192]{1,0:T(8,128)(2,1)S(1)} %copy-done.1, bf16[1,8192,512]{2,1,0:T(8,128)(2,1)} %param.24, f32[128,512]{1,0:T(8,128)S(1)} %fusion.3), kind=kOutput, calls=%fused_computation.1 | convolution fusion | flops 2148925440 | bytes 21233664 | tf_op jit(solution)/shard_map/dot_general | solution.py:469
  220.6 35.7 %shard_map.131 = f32[16,8192]{1,0:T(8,128)} custom-call(bf16[128,8192]{1,0:T(8,128)(2,1)} %convolution_convert_fusion.p_ref), custom_call_target="tpu_custom_call" | custom-call | tf_op jit(solution)/shard_map/pallas_call | solution.py:257
  256.4 0.2 fusion.18
  256.6 1.2 multiply_convert_fusion
  257.8 8.4 %all_to_all.15 = bf16[16,4,2048]{2,0,1:T(8,128)(2,1)S(1)} all-to-all(bf16[16,4,2048]{2,0,1:T(8,128)(2,1)S(1)} %bitcast.46), channel_id=1, replica_groups=mesh['seq'=8,'exp'=4] {'exp'}, dimensions={1} | all-to-all | bytes 524288 | tf_op jit(solution)/shard_map/all_to_all | solution.py:473
  266.2 3.6 %fusion.8 = bf16[512,2048]{1,0:T(8,128)(2,1)} fusion(bf16[512,2048]{1,0:T(8,128)(2,1)} %copy-done.2, bf16[64,2048]{1,0:T(8,128)(2,1)S(1)} %bitcast.45, s32[64]{0:T(128)S(1)} %eq.47, pred[64]{0:T(512)(128)(4,1)S(1)} %and.32), kind=kOutput, calls=%fused_computation.13 | convolution fusion | flops 137428992 | bytes 4456768 | tf_op jit(solution)/shard_map/dot_general | solution.py:479
  (6 shorter events, 0.0 us)
Async XLA Ops:
  0.0 256.4 %copy-start = (bf16[8192,1]{0,1:T(2,128)(2,1)S(1)}, bf16[8192,1]{0,1:T(2,128)(2,1)}, u32[]{:S(2)}) copy-start(bf16[8192,1]{0,1:T(2,128)(2,1)} %param.22) | copy-start | bytes 49156
  152.6 12.1 %copy-start.2 = (bf16[512,2048]{1,0:T(8,128)(2,1)}, bf16[512,2048]{1,0:T(8,128)(2,1)S(1)}, u32[]{:S(2)}) copy-start(bf16[512,2048]{1,0:T(8,128)(2,1)S(1)} %get-tuple-element.16) | copy-start | bytes 6291460
  205.6 5.4 %copy-start.1 = (bf16[128,8192]{1,0:T(8,128)(2,1)S(1)}, bf16[128,8192]{1,0:T(8,128)(2,1)}, u32[]{:S(2)}) copy-start(bf16[128,8192]{1,0:T(8,128)(2,1)} %shard_map.130) | copy-start | bytes 6291460

commit v3 on v2

--- a/solution.py
+++ b/solution.py
@@ -166,66 +166,74 @@
     return z, x, along, {"seq": z * 2 + 1 - x}
 
 
-def rows_kernel(nz, ne, cap, width, r_ref, o_ref, e_send, e_recv, z_send, z_recv, x_send, x_recv, own):
+def ring_device(pos, n):
+    half = pos // (n // 2)
+    return (1 - half) * pos * 2 + half * ((n - 1 - pos) * 2 + 1)
+
+
+def rows_kernel(n, ne, cap, width, r_ref, o_ref, e_send, e_recv, s_send, s_recv, own):
     me = lax.axis_index("seq")
     place = lax.axis_index("exp")
-    z, x, along, partner = lines(me, nz)
+    z, x = me // 2, lax.rem(me, 2)
+    pos = (1 - x) * z + x * (n - 1 - z)
+    ways = (1, n - 1)
+    nexts = [{"seq": ring_device(lax.rem(pos + way, n), n)} for way in ways]
     others = [{"exp": lax.rem(place + i, ne)} for i in range(1, ne)]
-    greet(others + along + [partner])
-
-    def piece(z_at, exp_at):
-        return o_ref.at[cut((z_at * 2 + x) * cap, cap), cut(exp_at * width, width)]
-
-    local = pltpu.make_async_copy(r_ref.at[cut(place * cap, cap), :], piece(z, place), own)
+    greet(others + nexts)
+
+    def piece(seq_at, exp_at):
+        return o_ref.at[cut(seq_at * cap, cap), cut(exp_at * width, width)]
+
+    local = pltpu.make_async_copy(r_ref.at[cut(place * cap, cap), :], piece(me, place), own)
     local.start()
     first = []
     for i in range(1, ne):
         src = r_ref.at[cut(lax.rem(place + i, ne) * cap, cap), :]
-        first.append(push(src, piece(z, place), e_send.at[i], e_recv.at[i], others[i - 1]))
-    second = []
-    third = []
+        first.append(push(src, piece(me, place), e_send.at[i], e_recv.at[i], others[i - 1]))
+    hops = {}
+    for t in range(n // 2):
+        for i in range(ne):
+            if t == 0:
+                local.wait() if i == 0 else first[i - 1].wait_recv()
+            for d in range(2):
+                if t:
+                    hops[i, d, t - 1].wait_recv()
+                if t == n // 2 - 1 and i % 2 != d:
+                    continue
+                seq_at = ring_device(lax.rem(pos + n + t * (ways[1 - d]), n), n)
+                part = piece(seq_at, lax.rem(place + ne - i, ne))
+                at = (i * 2 + d) * (n // 2) + t
+                hops[i, d, t] = push(part, part, s_send.at[at], s_recv.at[at], nexts[d])
     for i in range(ne):
-        if i == 0:
-            local.wait()
-        else:
-            first[i - 1].wait_recv()
-        part = piece(z, lax.rem(place + ne - i, ne))
-        for k in range(1, nz):
-            at = i * nz + k
-            second.append(push(part, part, z_send.at[at], z_recv.at[at], along[k - 1]))
-        third.append(push(part, part, x_send.at[i * nz], x_recv.at[i * nz], partner))
-    for k in range(1, nz):
-        for i in range(ne):
-            second[i * (nz - 1) + k - 1].wait_recv()
-            at = i * nz + k
-            part = piece(lax.rem(z + nz - k, nz), lax.rem(place + ne - i, ne))
-            third.append(push(part, part, x_send.at[at], x_recv.at[at], partner))
-    for copy in third:
-        copy.wait_recv()
-    for copy in first + second + third:
+        hops[i, i % 2, n // 2 - 1].wait_recv()
+    for copy in first + list(hops.values()):
         copy.wait_send()
 
 
 def share_rows(rows, n, ne):
     cap, width = rows.shape[0] // ne, rows.shape[1]
-    nz = n // 2
     anywhere = pl.BlockSpec(memory_space=pl.ANY)
     return pl.pallas_call(
-        functools.partial(rows_kernel, nz, ne, cap, width),
+        functools.partial(rows_kernel, n, ne, cap, width),
         out_shape=jax.ShapeDtypeStruct((n * cap, ne * width), rows.dtype),
         in_specs=[anywhere],
         out_specs=anywhere,
         scratch_shapes=[pltpu.SemaphoreType.DMA((ne,))] * 2
-        + [pltpu.SemaphoreType.DMA((ne * nz,))] * 4
+        + [pltpu.SemaphoreType.DMA((ne * n,))] * 2
         + [pltpu.SemaphoreType.DMA(())],
         compiler_params=pltpu.CompilerParams(collective_id=2, has_side_effects=True),
     )(rows)
 
 
-def sums_kernel(nz, cap, p_ref, o_ref, x_buf, s_buf, z_buf, x_send, x_recv, z_send, z_recv):
+def sums_kernel(
+    nz, ne, cap, p_ref, g_ref, o_ref, x_buf, s_buf, z_buf, total, w_buf,
+    x_send, x_recv, z_send, z_recv, e_send, e_recv, own,
+):
     me = lax.axis_index("seq")
     z, x, along, partner = lines(me, nz)
-    greet(along + [partner])
+    place = lax.axis_index("exp")
+    others = [{"exp": lax.rem(place + i, ne)} for i in range(1, ne)]
+    greet(along + [partner] + others)
 
     def rows_of(k, side):
         return cut((lax.rem(z + k, nz) * 2 + side) * cap, cap)
@@ -242,26 +250,42 @@
             s_buf[k] = both.astype(jnp.bfloat16)
             sent.append(push(s_buf.at[k], z_buf.at[k], z_send.at[k], z_recv.at[k], along[k - 1]))
         else:
-            o_ref[...] = both
+            total[...] = both
     for k in range(1, nz):
         sent[k - 1].wait_recv()
-        o_ref[...] += z_buf[k].astype(jnp.float32)
-    for copy in list(pairs.values()) + sent:
+        total[...] += z_buf[k].astype(jnp.float32)
+    w_buf[...] = (g_ref[...] * total[...]).astype(jnp.bfloat16)
+    width = w_buf.shape[1] // ne
+    mine = o_ref.at[cut(place * cap, cap), :]
+    local = pltpu.make_async_copy(w_buf.at[:, cut(place * width, width)], mine, own)
+    local.start()
+    spread = []
+    for i in range(1, ne):
+        src = w_buf.at[:, cut(lax.rem(place + i, ne) * width, width)]
+        spread.append(push(src, mine, e_send.at[i], e_recv.at[i], others[i - 1]))
+    local.wait()
+    for copy in spread:
+        copy.wait_recv()
+    for copy in list(pairs.values()) + sent + spread:
         copy.wait_send()
 
 
-def sum_rows(partial, n):
+def sum_rows(partial, gate, n, ne):
     cap, width = partial.shape[0] // n, partial.shape[1]
     nz = n // 2
     slots = pltpu.VMEM((nz, cap, width), jnp.bfloat16)
     return pl.pallas_call(
-        functools.partial(sums_kernel, nz, cap),
-        out_shape=jax.ShapeDtypeStruct((cap, width), jnp.float32),
-        in_specs=[pl.BlockSpec(memory_space=pltpu.VMEM)],
-        out_specs=pl.BlockSpec(memory_space=pltpu.VMEM),
-        scratch_shapes=[slots, slots, slots] + [pltpu.SemaphoreType.DMA((nz,))] * 4,
+        functools.partial(sums_kernel, nz, ne, cap),
+        out_shape=jax.ShapeDtypeStruct((ne * cap, width // ne), jnp.bfloat16),
+        in_specs=[pl.BlockSpec(memory_space=pltpu.VMEM)] * 2,
+        out_specs=pl.BlockSpec(memory_space=pl.ANY),
+        scratch_shapes=[slots, slots, slots]
+        + [pltpu.VMEM((cap, width), jnp.float32), pltpu.VMEM((cap, width), jnp.bfloat16)]
+        + [pltpu.SemaphoreType.DMA((nz,))] * 4
+        + [pltpu.SemaphoreType.DMA((ne,))] * 2
+        + [pltpu.SemaphoreType.DMA(())],
         compiler_params=pltpu.CompilerParams(collective_id=3, has_side_effects=True),
-    )(partial)
+    )(partial, gate)
 
 
 def flash_kernel(block, border_ref, q_ref, k_ref, v_ref, o_ref):
@@ -465,13 +489,8 @@
     gate_part = jnp.dot(piece, w_gate[0], preferred_element_type=jnp.float32)
     up_part = jnp.dot(piece, w_up[0], preferred_element_type=jnp.float32)
     inner_act = (jax.nn.silu(gate_part) * up_part).astype(jnp.bfloat16)
-    summed = sum_rows(
-        jnp.dot(inner_act, w_down[0], preferred_element_type=jnp.float32).astype(jnp.bfloat16), n_seq
-    )
-    weighted = (jax.nn.sigmoid(logits)[:, None] * summed).astype(jnp.bfloat16)
-    sliced = weighted.reshape(capacity, n_exp, D // n_exp)
-    returned = lax.all_to_all(sliced, "exp", split_axis=1, concat_axis=0, tiled=True)
-    returned = returned.reshape(n_exp * capacity, D // n_exp)
+    partial = jnp.dot(inner_act, w_down[0], preferred_element_type=jnp.float32).astype(jnp.bfloat16)
+    returned = sum_rows(partial, jax.nn.sigmoid(logits)[:, None], n_seq, n_exp)
     placing = (
         (jnp.arange(tokens, dtype=jnp.int32)[:, None] == local_index.reshape(1, -1))
         & filled.reshape(1, -1)

time: 270 us -> 254 us (0.941)
  blocking collectives: 14.6 us -> 6.25 us
  Pallas kernels: 210 us -> 202 us
    all_to_all x1 -> x0, blocking collectives: 8.39 us -> none  [shards(): lax.all_to_all(sliced, 'exp', split_axis=1, concat_axis=0, tiled=True)]
    pallas_call x2, Pallas kernels: 76.6 us -> 69.5 us  [the longest x1 37.7 us: sum_rows(): pl.pallas_call(functools.partial(sums_kernel, nz, ne, cap), out_shape=jax...]
where the time goes in v3:
time: 254 us; the launch traced here: 251 us
  Pallas kernels  202 us (80%)
  matrix products  33.1 us (13%)
  other arithmetic  6.28 us (2%)
  blocking collectives  6.25 us (2%)
  local copies, waits for them, and re-layouts  3.85 us (2%)
    pallas_call x1, Pallas kernels, heads_out(): pl.pallas_call(functools.partial(heads_out_kernel, n, width), out_shape=(...  57.4 us
    pallas_call x1, Pallas kernels, heads_back(): pl.pallas_call(functools.partial(heads_back_kernel, n, ny, width), out_sh...  53.4 us
    pallas_call x1, Pallas kernels, sum_rows(): pl.pallas_call(functools.partial(sums_kernel, nz, ne, cap), out_shape=jax...  37.7 us
    pallas_call x1, Pallas kernels, share_rows(): pl.pallas_call(functools.partial(rows_kernel, n, ne, cap, width), out_sha...  31.9 us
    pallas_call x1, Pallas kernels, flash(): pl.pallas_call(functools.partial(flash_kernel, block), out_shape=jax.Shap...  21.2 us
    dot_general x1, matrix products, shards(): mixed = jnp.dot(attended, out_proj, preferred_element_type=jnp.float32)  14.2 us
    dot_general x1, matrix products, shards(): jnp.dot(inner_act, w_down[0], preferred_element_type=jnp.float32)  9.6 us
    psum x1, blocking collectives, shards(): square_total = lax.psum(jnp.sum(hidden_wide * hidden_wide, axis=1), 'exp')  6.25 us

profile of v3, /device:TPU:0, one launch (start us, length us, event | category | flops | bytes accessed | tf_op | source)
XLA Modules:
  0.0 251.1 jit_solution(14878014823164839420)
XLA Ops:
  0.0 0.0 copy-start
  0.0 0.7 fusion.38
  0.7 0.2 reduce_window_sum.11
  0.9 0.7 broadcast_add_fusion
  1.6 0.1 select_reduce_fusion
  1.8 0.1 reshape.70
  1.9 57.4 %shard_map.127 = (bf16[4096,128]{1,0:T(8,128)(2,1)}, bf16[4096,128]{1,0:T(8,128)(2,1)}, bf16[4096,128]{1,0:T(8,128)(2,1)}) custom-call(bf16[512,1024]{1,0:T(8,128)(2,1)} %q_ref.1, bf16[512,1024]{1,0:T(8,128)(2,1)} %k_ref.1, bf16[512,1024]{1,0:T(8,128)(2,1)} %v_ref.1), custom_call_target="tpu_custom_call" | custom-call | tf_op jit(solution)/shard_map/pallas_call | solution.py:68
  59.3 1.3 convert_reduce_fusion
  60.6 21.2 %shard_map.128.a_ref = bf16[4096,128]{1,0:T(8,128)(2,1)} custom-call(s32[1]{0:T(128)} %bitcast.border_ref, bf16[4096,128]{1,0:T(8,128)(2,1)} %get-tuple-element.8.q_ref, bf16[4096,128]{1,0:T(8,128)(2,1)} %get-tuple-element.9.k_ref, bf16[4096,128]{1,0:T(8,128)(2,1)} %get-tuple-element.10.v_ref), custom_call_target="tpu_custom_call" | custom-call | tf_op jit(solution)/shard_map/pallas_call | solution.py:340
  81.8 53.4 %shard_map.129 = bf16[512,4096]{1,0:T(8,128)(2,1)} custom-call(bf16[4096,128]{1,0:T(8,128)(2,1)} %shard_map.128.a_ref), custom_call_target="tpu_custom_call" | custom-call | tf_op jit(solution)/shard_map/pallas_call | solution.py:137
  135.2 0.0 copy-start.3
  135.2 0.0 copy-start.4
  135.2 14.2 %fusion.5 = (f32[512]{0:T(512)S(1)}, bf16[512,2048]{1,0:T(8,128)(2,1)S(1)}) fusion(bf16[512,4096]{1,0:T(8,128)(2,1)} %shard_map.129, bf16[4096,2048]{1,0:T(8,128)(2,1)} %param.18, bf16[512,2048]{1,0:T(8,128)(2,1)} %param.13), kind=kOutput, calls=%fused_computation.10 | convolution fusion | flops 8596226048 | bytes 25167872 | tf_op jit(solution)/shard_map/dot_general | solution.py:465
  149.4 0.0 copy-start.2
  149.4 6.2 %psum.7 = f32[512]{0:T(512)S(1)} all-reduce(f32[512]{0:T(512)S(1)} %get-tuple-element.15), channel_id=1, replica_groups=mesh['seq'=8,'exp'=4] {'exp'}, use_global_device_ids=true, to_apply=%region_5.6 | all-reduce | flops 512 | bytes 4096 | tf_op jit(solution)/shard_map/psum | solution.py:472
  155.7 0.0 copy-done.3
  155.7 0.0 copy-done.4
  155.7 2.2 fusion.7
  157.9 2.8 %gather_fusion = bf16[64,2048]{1,0:T(8,128)(2,1)S(1)} fusion(bf16[512,2048]{1,0:T(8,128)(2,1)} %fusion.7, s32[1024]{0:T(1024)S(1)} %pad_clamp_fusion), kind=kCustom, calls=%fused_computation | custom fusion | bytes 524544 | tf_op jit(solution)/shard_map/jit(_take)/gather | solution.py:484
  160.7 0.1 eq.47
  160.8 0.1 fusion.34
  161.0 0.1 and.32
  161.1 0.8 select_select_fusion.r_ref
  161.9 31.9 %shard_map.130 = bf16[128,8192]{1,0:T(8,128)(2,1)} custom-call(bf16[64,2048]{1,0:T(8,128)(2,1)} %select_select_fusion.r_ref), custom_call_target="tpu_custom_call" | custom-call | tf_op jit(solution)/shard_map/pallas_call | solution.py:216
  193.8 0.0 copy-start.1
  193.8 5.4 %fusion.3 = f32[128,512]{1,0:T(8,128)S(1)} fusion(bf16[128,8192]{1,0:T(8,128)(2,1)} %shard_map.130, bf16[1,8192,512]{2,1,0:T(8,128)(2,1)} %param.23), kind=kOutput, calls=%fused_computation.5 | convolution fusion | flops 1073741824 | bytes 10747904 | tf_op jit(solution)/shard_map/dot_general | solution.py:489
  199.2 9.6 %convolution_convert_fusion.p_ref = bf16[128,8192]{1,0:T(8,128)(2,1)} fusion(bf16[1,512,8192]{2,1,0:T(8,128)(2,1)} %param.25, bf16[128,8192]{1,0:T(8,128)(2,1)S(1)} %copy-done.1, bf16[1,8192,512]{2,1,0:T(8,128)(2,1)} %param.24, f32[128,512]{1,0:T(8,128)S(1)} %fusion.3), kind=kOutput, calls=%fused_computation.1 | convolution fusion | flops 2148925440 | bytes 21233664 | tf_op jit(solution)/shard_map/dot_general | solution.py:492
  208.8 0.0 copy-done
  208.8 0.2 fusion.19
  209.0 0.7 copy.15.g_ref
  209.7 37.7 %shard_map.131 = bf16[64,2048]{1,0:T(8,128)(2,1)} custom-call(bf16[128,8192]{1,0:T(8,128)(2,1)} %convolution_convert_fusion.p_ref, f32[16,1]{1,0:T(8,128)} %copy.15.g_ref), custom_call_target="tpu_custom_call" | custom-call | tf_op jit(solution)/shard_map/pallas_call | solution.py:277
  247.4 3.7 %fusion.8 = bf16[512,2048]{1,0:T(8,128)(2,1)} fusion(bf16[512,2048]{1,0:T(8,128)(2,1)} %copy-done.2, bf16[64,2048]{1,0:T(8,128)(2,1)} %shard_map.131, s32[64]{0:T(128)S(1)} %eq.47, pred[64]{0:T(512)(128)(4,1)S(1)} %and.32), kind=kOutput, calls=%fused_computation.13 | convolution fusion | flops 137428992 | bytes 4456768 | tf_op jit(solution)/shard_map/dot_general | solution.py:498
  (8 shorter events, 0.1 us)
Async XLA Ops:
  0.0 208.8 %copy-start = (bf16[8192,1]{0,1:T(2,128)(2,1)S(1)}, bf16[8192,1]{0,1:T(2,128)(2,1)}, u32[]{:S(2)}) copy-start(bf16[8192,1]{0,1:T(2,128)(2,1)} %param.22) | copy-start | bytes 49156
  135.2 20.5 %copy-start.3 = (f32[2,2048]{1,0:T(2,128)S(1)}, f32[2,2048]{1,0:T(2,128)}, u32[]{:S(2)}) copy-start(f32[2,2048]{1,0:T(2,128)} %param.20) | copy-start | bytes 49156
  135.2 20.5 %copy-start.4 = (s32[512]{0:T(512)S(1)}, s32[512]{0:T(512)}, u32[]{:S(2)}) copy-start(s32[512]{0:T(512)} %param.19) | copy-start | bytes 6148
  149.4 12.5 %copy-start.2 = (bf16[512,2048]{1,0:T(8,128)(2,1)}, bf16[512,2048]{1,0:T(8,128)(2,1)S(1)}, u32[]{:S(2)}) copy-start(bf16[512,2048]{1,0:T(8,128)(2,1)S(1)} %get-tuple-element.16) | copy-start | bytes 6291460
  193.8 5.4 %copy-start.1 = (bf16[128,8192]{1,0:T(8,128)(2,1)S(1)}, bf16[128,8192]{1,0:T(8,128)(2,1)}, u32[]{:S(2)}) copy-start(bf16[128,8192]{1,0:T(8,128)(2,1)} %shard_map.130) | copy-start | bytes 6291460
